TPU v7x, 32 devices: a whole 2x2x4 slice. The times are simulated.
32 devices in a mesh: area: 4 (over y, core), depth: 8 (over z, x).
Axes of the slice: x: 2, y: 2, z: 4, core: 2. Of those that a mesh axis runs over, the one named last changes fastest.
Arguments:
- field: float32 [256, 256, 512], P('depth', 'area'), may hold values from -6 to 6
- materials: int32 [256, 256, 512], P('depth', 'area'), may hold values from 0 to 15
- tf_table: float32 [4, 16], replicated, may hold values from 0 to 1, as said below
- view_order: int32 [2, 8], replicated, may hold values from 0 to 7, each once within a row
- shear_offset: int32 [8], replicated, may hold values from 0 to 63, as said below
Outputs:
- image: float32 [2, 4, 256, 512], P(None, None, ('area', 'depth'))
Inputs may be any that keep to these rules, and one draw needn't show every extreme that they name: `shear_offset`: every entry lies in 0 to 63; some layer has offset 0 and some layer has offset 64 - 1. `view_order`: each row is a permutation of the depth layers. `tf_table`: the colour rows lie in 0.05 to 0.6; the opacity row lies in 0.02 / 32 to 0.5 / 32.
All inputs are finite; a program needn't handle non-finite values.
Results may differ from a plain program's by a relative error of at most 0.0003.
Values sent between devices are 32-bit elements; how exact they have to be, the bound alone decides.
No kernel may reach another device: no remote copies, remote signals or barrier semaphores. Data moves between devices by JAX's collectives and lax.ppermute only.
A program may use at most 128 MiB of HBM per device.

v0:
```python
import functools

import jax
import jax.numpy as jnp
from jax import lax
from jax.experimental import pallas as pl
from jax.experimental.pallas import tpu as pltpu
from jax.sharding import PartitionSpec as P

LANES, SUB = 128, 8
LOG2E = 1.4426950408889634
SHADE_UNIT = 0.7 * 0.5 * 0.48

LOOKUP = lax.GatherDimensionNumbers(
    offset_dims=(),
    collapsed_slice_dims=(1,),
    start_index_map=(1,),
    operand_batching_dims=(0,),
    start_indices_batching_dims=(0,),
)


def lookup(table, idx):
    return lax.gather(
        table, idx[:, :, None], LOOKUP, (1, 1), mode=lax.GatherScatterMode.PROMISE_IN_BOUNDS
    )


def put(ref, tile, channel, cols, value):
    own = ref.shape[2]
    if own >= SUB:
        per = own // SUB
        if per == 1:
            ref[tile, channel, :, cols] = value
        else:
            ref[tile // per, channel, pl.ds(pl.multiple_of((tile % per) * SUB, SUB), SUB), cols] = value
    else:
        for part in range(SUB // own):
            ref[tile * (SUB // own) + part, channel, :, cols] = value[part * own : (part + 1) * own]


def march_body(
    offset, field_hbm, mats_hbm, z_lo, z_hi, y_lo, y_hi, table,
    first, own, spill, field, mats, weight, keep, spread, sems,
):
    depth, rows, width = field_hbm.shape
    strips = width // LANES
    cols = [slice(j * LANES, (j + 1) * LANES) for j in range(strips)]
    copies = []
    for j in range(strips):
        lanes = pl.ds(j * LANES, LANES)
        copies.append(
            pltpu.make_async_copy(
                field_hbm.at[:, :, lanes],
                field.at[pl.ds(1, depth), j, pl.ds(SUB, rows), :],
                sems.at[0, j],
            )
        )
        copies.append(pltpu.make_async_copy(mats_hbm.at[:, :, lanes], mats.at[:, j], sems.at[1, j]))
    for copy in copies:
        copy.start()
    for j in range(strips):
        field[0, j, SUB : SUB + rows, :] = z_lo[:, cols[j]]
        field[depth + 1, j, SUB : SUB + rows, :] = z_hi[:, cols[j]]
    spread[...] = jnp.zeros_like(spread)
    for copy in copies:
        copy.wait()
    for j in range(strips):
        field[1 : depth + 1, j, SUB - 1, :] = y_lo[:, cols[j]]
        field[1 : depth + 1, j, SUB + rows, :] = y_hi[:, cols[j]]
    lane = lax.broadcasted_iota(jnp.int32, (SUB, LANES), 1)
    left_end = lane == 0
    right_end = lane == LANES - 1
    zero = jnp.zeros((SUB, LANES), jnp.float32)
    shift = offset[0]

    def tile(i, unused):
        r = pl.multiple_of(i * SUB, SUB)
        opacity_row = jnp.broadcast_to(table[3:4, :], (SUB, LANES))

        def cells(z, unused):
            f = [field[z + 1, j, pl.ds(SUB + r, SUB), :] for j in range(strips)]
            from_left = [pltpu.roll(v, 1, 1) for v in f]
            from_right = [pltpu.roll(v, LANES - 1, 1) for v in f]
            for j in range(strips):
                above = field[z + 2, j, pl.ds(SUB + r, SUB), :]
                below = field[z, j, pl.ds(SUB + r, SUB), :]
                dz = above - below
                dy = (
                    field[z + 1, j, pl.ds(SUB + r + 1, SUB), :]
                    - field[z + 1, j, pl.ds(SUB + r - 1, SUB), :]
                )
                left = jnp.where(left_end, from_left[j - 1] if j else zero, from_left[j])
                right = jnp.where(
                    right_end, from_right[j + 1] if j < strips - 1 else zero, from_right[j]
                )
                dx = right - left
                grad_sq = 0.25 * (dz * dz + dy * dy + dx * dx)
                slope = jnp.abs(dz + (0.6 / 0.48) * dy + (0.64 / 0.48) * dx)
                shade = (0.3 / SHADE_UNIT) + slope * lax.rsqrt(grad_sq + 1.0)
                clear = jnp.exp2((-0.25 * LOG2E) * (f[j] * f[j] + grad_sq))
                most = lookup(opacity_row, mats[z, j, pl.ds(r, SUB), :])
                opacity = most - most * clear
                weight[z, j] = shade * opacity
                keep[z, j] = 1.0 - opacity
            return unused

        lax.fori_loop(0, depth, cells, 0, unroll=8)
        for j0 in range(0, strips, 2):
            colours = [jnp.broadcast_to(table[c : c + 1, :], (SUB, LANES)) for c in range(3)]

            def step(z, carry):
                result = []
                for k, (passed, front, back) in enumerate(carry):
                    j = j0 + k
                    w = weight[z, j]
                    kept = keep[z, j]
                    seen = w * passed
                    idx = mats[z, j, pl.ds(r, SUB), :]
                    looked = [lookup(t, idx) for t in colours]
                    result.append(
                        (
                            passed * kept,
                            [front[c] + looked[c] * seen for c in range(3)],
                            [back[c] * kept + looked[c] * w for c in range(3)],
                        )
                    )
                return result

            start = [(zero + 1.0, [zero] * 3, [zero] * 3)] * 2
            done = lax.fori_loop(0, depth, step, start, unroll=8)
            for k, (passed, front, back) in enumerate(done):
                j = j0 + k
                place = pl.ds(shift + r, SUB)
                for c in range(3):
                    put(first, i, c, cols[j], front[c])
                    spread[c, j, place, :] = back[c]
                put(first, i, 3, cols[j], 1.0 - passed)
                spread[3, j, place, :] = 1.0 - passed
        return unused

    lax.fori_loop(0, rows // SUB, tile, 0)

    def hand_out(i, unused):
        r = pl.multiple_of(i * SUB, SUB)
        for c in range(4):
            for j in range(strips):
                put(own, i, c, cols[j], spread[c, j, pl.ds(r, SUB), :])
                put(spill, i, c, cols[j], spread[c, j, pl.ds(rows + r, SUB), :])
        return unused

    lax.fori_loop(0, rows // SUB, hand_out, 0)


def march(offset, field, mats, z_lo, z_hi, y_lo, y_hi, table, receivers):
    depth, rows, width = field.shape
    strips = width // LANES
    vmem = pl.BlockSpec(memory_space=pltpu.VMEM)
    hbm = pl.BlockSpec(memory_space=pltpu.HBM)
    image = jax.ShapeDtypeStruct((receivers, 4, rows // receivers, width), jnp.float32)
    return pl.pallas_call(
        march_body,
        out_shape=(image, image, image),
        in_specs=[pl.BlockSpec(memory_space=pltpu.SMEM), hbm, hbm] + [vmem] * 5,
        out_specs=(vmem, vmem, vmem),
        scratch_shapes=[
            pltpu.VMEM((depth + 2, strips, rows + 2 * SUB, LANES), jnp.float32),
            pltpu.VMEM((depth, strips, rows, LANES), jnp.int32),
            pltpu.VMEM((depth, strips, SUB, LANES), jnp.float32),
            pltpu.VMEM((depth, strips, SUB, LANES), jnp.float32),
            pltpu.VMEM((4, strips, 2 * rows, LANES), jnp.float32),
            pltpu.SemaphoreType.DMA((2, strips)),
        ],
        compiler_params=pltpu.CompilerParams(vmem_limit_bytes=40 << 20),
        cost_estimate=pl.CostEstimate(flops=10**8, bytes_accessed=10**7, transcendentals=10**6),
        name="march",
    )(offset, field, mats, z_lo, z_hi, y_lo, y_hi, table)


def composite_body(order, *refs):
    out = refs[-1]
    for view, stack in enumerate(refs[:-1]):
        layers = stack.shape[0]
        seen = jnp.ones(stack.shape[2:], jnp.float32)
        colour = [jnp.zeros(stack.shape[2:], jnp.float32)] * 3
        for k in range(layers):
            layer = order[view, k]
            colour = [colour[c] + seen * stack[layer, c] for c in range(3)]
            seen = seen - seen * stack[layer, 3]
        for c in range(3):
            out[view, c] = colour[c]
        out[view, 3] = 1.0 - seen


def composite(order, stacks):
    vmem = pl.BlockSpec(memory_space=pltpu.VMEM)
    return pl.pallas_call(
        composite_body,
        out_shape=jax.ShapeDtypeStruct((len(stacks),) + stacks[0].shape[1:], jnp.float32),
        in_specs=[pl.BlockSpec(memory_space=pltpu.SMEM)] + [vmem] * len(stacks),
        out_specs=vmem,
        name="composite",
    )(order, *stacks)


def neighbours(block, axis, dim):
    count = lax.axis_size(axis)
    up = [(i, i + 1) for i in range(count - 1)]
    down = [(b, a) for a, b in up]
    size = block.shape[dim]
    low = lax.ppermute(lax.index_in_dim(block, size - 1, dim, keepdims=False), axis, up)
    high = lax.ppermute(lax.index_in_dim(block, 0, dim, keepdims=False), axis, down)
    return low, high


def shards(field, materials, tf_table, view_order, shear_offset):
    receivers = lax.axis_size("depth")
    y_lo, y_hi = neighbours(field, "area", 1)
    z_lo, z_hi = neighbours(field, "depth", 0)
    scaled = tf_table * jnp.array([[SHADE_UNIT]] * 3 + [[1.0]], jnp.float32)
    table = jnp.pad(scaled, ((0, 0), (0, LANES - tf_table.shape[1])))
    offset = lax.dynamic_slice_in_dim(shear_offset, lax.axis_index("depth"), 1)
    first, own, spill = march(offset, field, materials, z_lo, z_hi, y_lo, y_hi, table, receivers)
    columns = lax.axis_size("area")
    stack0 = lax.all_to_all(first, "depth", split_axis=0, concat_axis=0, tiled=True)
    arrived = lax.ppermute(spill, "area", [(i, i + 1) for i in range(columns - 1)])
    sheared = own + arrived
    stack1 = lax.all_to_all(sheared, "depth", split_axis=0, concat_axis=0, tiled=True)
    return composite(view_order, (stack0, stack1))


def solution(mesh):
    in_specs = (P("depth", "area", None), P("depth", "area", None), P(), P(), P())
    out_specs = P(None, None, ("area", "depth"), None)
    return jax.shard_map(shards, mesh=mesh, in_specs=in_specs, out_specs=out_specs, check_vma=False)
```

profile of v0, /device:TPU:0, one launch (start us, length us, event | category | flops | bytes accessed | tf_op | source)
XLA Modules:
  0.0 84.5 jit_solution(15692488631097818698)
XLA Ops:
  0.0 1.3 %fusion = (f32[32,1,512]{2,1,0:T(1,128)S(1)}, f32[32,1,512]{2,1,0:T(1,128)S(1)}) fusion(f32[32,64,512]{2,1,0:T(8,128)} %field_hbm.1), kind=kLoop, calls=%fused_computation.5 | loop fusion | bytes 262144 | tf_op jit(solution)/shard_map/slice | solution.py:212
  1.3 2.4 %collective-permute-start.2 = (f32[32,512]{1,0:T(8,128)S(1)}, f32[32,512]{1,0:T(8,128)S(1)}, u32[]{:S(2)}, u32[]{:S(2)}) collective-permute-start(f32[32,512]{1,0:T(8,128)S(1)} %bitcast.10), channel_id=1, source_target_pairs={{0,8},{8,16},{16,24},{1,9},{9,17},{17,25},{2,10},{10,18},{18,26},{... | collective-permute-start | bytes 196616 | tf_op jit(solution)/shard_map/ppermute | solution.py:211
  3.8 1.3 %collective-permute-start.3 = (f32[32,512]{1,0:T(8,128)S(1)}, f32[32,512]{1,0:T(8,128)S(1)}, u32[]{:S(2)}, u32[]{:S(2)}) collective-permute-start(f32[32,512]{1,0:T(8,128)S(1)} %bitcast.11), channel_id=1, source_target_pairs={{8,0},{16,8},{24,16},{9,1},{17,9},{25,17},{10,2},{18,10},{26,18},{... | collective-permute-start | bytes 196616 | tf_op jit(solution)/shard_map/ppermute | solution.py:212
  5.1 1.0 %slice_bitcast_fusion = (f32[64,512]{1,0:T(8,128)S(1)}, f32[64,512]{1,0:T(8,128)S(1)}) fusion(f32[32,64,512]{2,1,0:T(8,128)} %field_hbm.1), kind=kLoop, calls=%fused_computation | loop fusion | bytes 524288 | tf_op jit(solution)/shard_map/squeeze | solution.py:212
  6.0 1.3 %collective-permute-start.1 = (f32[64,512]{1,0:T(8,128)S(1)}, f32[64,512]{1,0:T(8,128)S(1)}, u32[]{:S(2)}, u32[]{:S(2)}) collective-permute-start(f32[64,512]{1,0:T(8,128)S(1)} %get-tuple-element.13), channel_id=1, source_target_pairs={{1,0},{2,1},{3,2},{4,3},{5,4},{6,5},{7,6},{9,8},{10,9},{11,10},{12... | collective-permute-start | bytes 393224 | tf_op jit(solution)/shard_map/ppermute | solution.py:212
  7.3 4.8 %collective-permute-start = (f32[64,512]{1,0:T(8,128)S(1)}, f32[64,512]{1,0:T(8,128)S(1)}, u32[]{:S(2)}, u32[]{:S(2)}) collective-permute-start(f32[64,512]{1,0:T(8,128)S(1)} %get-tuple-element.14), channel_id=1, source_target_pairs={{0,1},{1,2},{2,3},{3,4},{4,5},{5,6},{6,7},{8,9},{9,10},{10,11},{11... | collective-permute-start | bytes 393224 | tf_op jit(solution)/shard_map/ppermute | solution.py:211
  12.2 0.8 broadcast_multiply_fusion
  13.0 1.2 %dynamic_slice.3.offset = s32[1]{0:T(128)} dynamic-slice(s32[8]{0:T(128)} %param.10, s32[]{:T(128)S(6)} %select_n.3), dynamic_slice_sizes={1} | dynamic-slice | bytes 12 | tf_op jit(solution)/shard_map/dynamic_slice | solution.py:222
  14.2 0.0 collective-permute-done.2.y_lo
  14.2 0.0 collective-permute-done.3.y_hi
  14.2 0.0 collective-permute-done.1.z_hi
  14.2 3.5 %collective-permute-done.z_lo = f32[64,512]{1,0:T(8,128)S(1)} collective-permute-done((f32[64,512]{1,0:T(8,128)S(1)}, f32[64,512]{1,0:T(8,128)S(1)}, u32[]{:S(2)}, u32[]{:S(2)}) %collective-permute-start) | collective-permute-done | bytes 131104 | tf_op jit(solution)/shard_map/ppermute | solution.py:211
  17.7 0.0 copy-start
  17.7 2.2 %copy-done = f32[32,64,512]{2,1,0:T(8,128)S(1)} copy-done((f32[32,64,512]{2,1,0:T(8,128)S(1)}, f32[32,64,512]{2,1,0:T(8,128)}, u32[]{:S(2)}) %copy-start) | copy-done | bytes 4194328
  19.9 0.0 copy-start.1
  19.9 2.2 %copy-done.1 = s32[32,64,512]{2,1,0:T(8,128)S(1)} copy-done((s32[32,64,512]{2,1,0:T(8,128)S(1)}, s32[32,64,512]{2,1,0:T(8,128)}, u32[]{:S(2)}) %copy-start.1) | copy-done | bytes 4194328
  22.1 21.3 %march.1 = (f32[8,4,8,512]{3,2,1,0:T(8,128)}, f32[8,4,8,512]{3,2,1,0:T(8,128)S(1)}, f32[8,4,8,512]{3,2,1,0:T(8,128)S(1)}) custom-call(s32[1]{0:T(128)} %dynamic_slice.3.offset, f32[32,64,512]{2,1,0:T(8,128)S(1)} %copy-done, s32[32,64,512]{2,1,0:T(8,128)S(1)} %copy-done.1, f32[64,512]{1,0:T(8,128)S(1)} %collective-permute-done.z_lo, ...), custom_call_target="tpu_custom_call" | custom-call | flops 100000000 | bytes 10000000 | tf_op jit(solution)/shard_map/march/pallas_call | solution.py:161
  43.4 5.9 %all-to-all-start = ((f32[8,4,8,512]{3,2,1,0:T(8,128)}), f32[8,4,8,512]{3,2,1,0:T(8,128)S(1)}, u32[]{:S(2)}, u32[]{:S(2)}) async-start(f32[8,4,8,512]{3,2,1,0:T(8,128)} %get-tuple-element.8), calls=%async_computation | async-start | bytes 1048576 | tf_op jit(solution)/shard_map/all_to_all | solution.py:225
  49.2 2.1 %collective-permute-start.4 = (f32[8,4,8,512]{3,2,1,0:T(8,128)S(1)}, f32[8,4,8,512]{3,2,1,0:T(8,128)S(1)}, u32[]{:S(2)}, u32[]{:S(2)}) collective-permute-start(f32[8,4,8,512]{3,2,1,0:T(8,128)S(1)} %get-tuple-element.10), channel_id=1, source_target_pairs={{0,8},{8,16},{16,24},{1,9},{9,17},{17,25},{2,10},{10,18},{18,26},{... | collective-permute-start | bytes 1572872 | tf_op jit(solution)/shard_map/ppermute | solution.py:226
  51.3 1.5 %collective-permute-done.4 = f32[8,4,8,512]{3,2,1,0:T(8,128)S(1)} collective-permute-done((f32[8,4,8,512]{3,2,1,0:T(8,128)S(1)}, f32[8,4,8,512]{3,2,1,0:T(8,128)S(1)}, u32[]{:S(2)}, u32[]{:S(2)}) %collective-permute-start.4) | collective-permute-done | bytes 524320 | tf_op jit(solution)/shard_map/ppermute | solution.py:226
  52.8 0.1 add.9
  52.9 11.4 %all-to-all-done.refs_0_ = f32[8,4,8,512]{3,2,1,0:T(8,128)S(1)} async-done(((f32[8,4,8,512]{3,2,1,0:T(8,128)}), f32[8,4,8,512]{3,2,1,0:T(8,128)S(1)}, u32[]{:S(2)}, u32[]{:S(2)}) %all-to-all-start) | async-done | bytes 524320 | tf_op jit(solution)/shard_map/all_to_all | solution.py:225
  64.3 0.0 copy-start.2
  64.3 18.2 %all_to_all.10.refs_1_ = f32[8,4,8,512]{3,2,1,0:T(8,128)} all-to-all(f32[8,4,8,512]{3,2,1,0:T(8,128)S(1)} %add.9), channel_id=1, replica_groups=mesh['area'=4,'depth'=8] {'depth'}, dimensions={0} | all-to-all | bytes 1048576 | tf_op jit(solution)/shard_map/all_to_all | solution.py:228
  82.6 0.0 copy-done.2
  82.6 1.9 %composite.1 = f32[2,4,8,512]{3,2,1,0:T(8,128)} custom-call(s32[2,8]{1,0:T(2,128)} %order.1, f32[8,4,8,512]{3,2,1,0:T(8,128)} %copy-done.2, f32[8,4,8,512]{3,2,1,0:T(8,128)} %all_to_all.10.refs_1_), custom_call_target="tpu_custom_call" | custom-call | tf_op jit(solution)/shard_map/composite/pallas_call | solution.py:197
  (3 shorter events, 0.0 us)
Async XLA Ops:
  1.3 12.9 %collective-permute-start.2 = (f32[32,512]{1,0:T(8,128)S(1)}, f32[32,512]{1,0:T(8,128)S(1)}, u32[]{:S(2)}, u32[]{:S(2)}) collective-permute-start(f32[32,512]{1,0:T(8,128)S(1)} %bitcast.10), channel_id=1, source_target_pairs={{0,8},{8,16},{16,24},{1,9},{9,17},{17,25},{2,10},{10,18},{18,26},{... | collective-permute-start | bytes 196616 | tf_op jit(solution)/shard_map/ppermute | solution.py:211
  3.8 10.5 %collective-permute-start.3 = (f32[32,512]{1,0:T(8,128)S(1)}, f32[32,512]{1,0:T(8,128)S(1)}, u32[]{:S(2)}, u32[]{:S(2)}) collective-permute-start(f32[32,512]{1,0:T(8,128)S(1)} %bitcast.11), channel_id=1, source_target_pairs={{8,0},{16,8},{24,16},{9,1},{17,9},{25,17},{10,2},{18,10},{26,18},{... | collective-permute-start | bytes 196616 | tf_op jit(solution)/shard_map/ppermute | solution.py:212
  6.0 8.2 %collective-permute-start.1 = (f32[64,512]{1,0:T(8,128)S(1)}, f32[64,512]{1,0:T(8,128)S(1)}, u32[]{:S(2)}, u32[]{:S(2)}) collective-permute-start(f32[64,512]{1,0:T(8,128)S(1)} %get-tuple-element.13), channel_id=1, source_target_pairs={{1,0},{2,1},{3,2},{4,3},{5,4},{6,5},{7,6},{9,8},{10,9},{11,10},{12... | collective-permute-start | bytes 393224 | tf_op jit(solution)/shard_map/ppermute | solution.py:212
  7.3 10.4 %collective-permute-start = (f32[64,512]{1,0:T(8,128)S(1)}, f32[64,512]{1,0:T(8,128)S(1)}, u32[]{:S(2)}, u32[]{:S(2)}) collective-permute-start(f32[64,512]{1,0:T(8,128)S(1)} %get-tuple-element.14), channel_id=1, source_target_pairs={{0,1},{1,2},{2,3},{3,4},{4,5},{5,6},{6,7},{8,9},{9,10},{10,11},{11... | collective-permute-start | bytes 393224 | tf_op jit(solution)/shard_map/ppermute | solution.py:211
  17.7 2.2 %copy-start = (f32[32,64,512]{2,1,0:T(8,128)S(1)}, f32[32,64,512]{2,1,0:T(8,128)}, u32[]{:S(2)}) copy-start(f32[32,64,512]{2,1,0:T(8,128)} %field_hbm.1) | copy-start | bytes 12582916
  19.9 2.2 %copy-start.1 = (s32[32,64,512]{2,1,0:T(8,128)S(1)}, s32[32,64,512]{2,1,0:T(8,128)}, u32[]{:S(2)}) copy-start(s32[32,64,512]{2,1,0:T(8,128)} %mats_hbm.1) | copy-start | bytes 12582916
  43.4 20.9 %all-to-all-start = ((f32[8,4,8,512]{3,2,1,0:T(8,128)}), f32[8,4,8,512]{3,2,1,0:T(8,128)S(1)}, u32[]{:S(2)}, u32[]{:S(2)}) async-start(f32[8,4,8,512]{3,2,1,0:T(8,128)} %get-tuple-element.8), calls=%async_computation | async-start | bytes 1048576 | tf_op jit(solution)/shard_map/all_to_all | solution.py:225
  49.2 3.6 %collective-permute-start.4 = (f32[8,4,8,512]{3,2,1,0:T(8,128)S(1)}, f32[8,4,8,512]{3,2,1,0:T(8,128)S(1)}, u32[]{:S(2)}, u32[]{:S(2)}) collective-permute-start(f32[8,4,8,512]{3,2,1,0:T(8,128)S(1)} %get-tuple-element.10), channel_id=1, source_target_pairs={{0,8},{8,16},{16,24},{1,9},{9,17},{17,25},{2,10},{10,18},{18,26},{... | collective-permute-start | bytes 1572872 | tf_op jit(solution)/shard_map/ppermute | solution.py:226
  64.3 18.2 %copy-start.2 = (f32[8,4,8,512]{3,2,1,0:T(8,128)}, f32[8,4,8,512]{3,2,1,0:T(8,128)S(1)}, u32[]{:S(2)}) copy-start(f32[8,4,8,512]{3,2,1,0:T(8,128)S(1)} %all-to-all-done.refs_0_) | copy-start | bytes 1572868
where the time goes:
time: 85 us; the launch traced here: 84.5 us
  Pallas kernels  23.2 us (27%)
  blocking collectives  18.2 us (21%)
  starting transfers between devices  17.8 us (21%)
  waiting for transfers between devices  16.4 us (19%)
  local copies, waits for them, and re-layouts  7.94 us (9%)
    pallas_call x1, Pallas kernels, march(): pl.pallas_call(march_body, out_shape=(image, image, image), in_specs=[pl....  21.3 us
    all_to_all x1, blocking collectives, shards(): lax.all_to_all(sheared, 'depth', split_axis=0, concat_axis=0, tiled=True)  18.2 us
    all_to_all x1, waiting for transfers between devices, shards(): lax.all_to_all(first, 'depth', split_axis=0, concat_axis=0, tiled=True)  11.4 us
    ppermute x2, starting transfers between devices, neighbours(): lax.ppermute(lax.index_in_dim(block, size - 1, dim, keepdims=False), axis...  7.25 us
    all_to_all x1, starting transfers between devices, shards(): lax.all_to_all(first, 'depth', split_axis=0, concat_axis=0, tiled=True)  5.85 us
    unnamed x8, local copies, waits for them, and re-layouts  4.39 us
    ppermute x2, waiting for transfers between devices, neighbours(): lax.ppermute(lax.index_in_dim(block, size - 1, dim, keepdims=False), axis...  3.52 us
    ppermute x2, starting transfers between devices, neighbours(): lax.ppermute(lax.index_in_dim(block, 0, dim, keepdims=False), axis, down)  2.58 us
  transfers between devices with their start and end apart: 6, of which 3 were waited for; matrix products, arithmetic and copies ran while one was open for 4% of the time, Pallas kernels for 0%

commit v1 on v0

v1 whole, which is shorter than its diff:
```python
import functools

import jax
import jax.numpy as jnp
from jax import lax
from jax.experimental import pallas as pl
from jax.experimental.pallas import tpu as pltpu
from jax.sharding import PartitionSpec as P

LANES, SUB, GROUP = 128, 8, 16
LOG2E = 1.4426950408889634
SHADE_UNIT = 0.7 * 0.5 * 0.48

LOOKUP = lax.GatherDimensionNumbers(
    offset_dims=(),
    collapsed_slice_dims=(0,),
    start_index_map=(0,),
    operand_batching_dims=(1,),
    start_indices_batching_dims=(1,),
)


def lookup(halves, idx):
    place = (idx & (SUB - 1))[:, :, None]
    low, high = (
        lax.gather(half, place, LOOKUP, (1, 1), mode=lax.GatherScatterMode.PROMISE_IN_BOUNDS)
        for half in halves
    )
    return jnp.where(idx >= SUB, high, low)


def put(ref, tile, channel, cols, value):
    own = ref.shape[2]
    if own >= SUB:
        per = own // SUB
        if per == 1:
            ref[tile, channel, :, cols] = value
        else:
            ref[tile // per, channel, pl.ds(pl.multiple_of((tile % per) * SUB, SUB), SUB), cols] = value
    else:
        for part in range(SUB // own):
            ref[tile * (SUB // own) + part, channel, :, cols] = value[part * own : (part + 1) * own]


def is_even(axis):
    return lax.rem(lax.axis_index(axis), 2) == 0


def edges_body(field_hbm, z_first, z_second, y_first, y_second, rim, sems):
    depth, rows, _ = field_hbm.shape
    z_even, y_even = is_even("depth"), is_even("area")
    copies = [
        pltpu.make_async_copy(field_hbm.at[jnp.where(z_even, depth - 1, 0)], z_first, sems.at[0]),
        pltpu.make_async_copy(field_hbm.at[jnp.where(z_even, 0, depth - 1)], z_second, sems.at[1]),
        pltpu.make_async_copy(field_hbm.at[:, pl.ds(0, SUB), :], rim.at[0], sems.at[2]),
        pltpu.make_async_copy(field_hbm.at[:, pl.ds(rows - SUB, SUB), :], rim.at[1], sems.at[3]),
    ]
    for copy in copies:
        copy.start()
    for copy in copies[2:]:
        copy.wait()
    low, high = rim[0, :, 0, :], rim[1, :, SUB - 1, :]
    y_first[...] = jnp.where(y_even, high, low)
    y_second[...] = jnp.where(y_even, low, high)
    for copy in copies[:2]:
        copy.wait()


def edges(field):
    depth, rows, width = field.shape
    vmem = pl.BlockSpec(memory_space=pltpu.VMEM)
    plane = jax.ShapeDtypeStruct((rows, width), jnp.float32)
    wall = jax.ShapeDtypeStruct((depth, width), jnp.float32)
    return pl.pallas_call(
        edges_body,
        out_shape=(plane, plane, wall, wall),
        in_specs=[pl.BlockSpec(memory_space=pltpu.HBM)],
        out_specs=(vmem,) * 4,
        scratch_shapes=[
            pltpu.VMEM((2, depth, SUB, width), jnp.float32),
            pltpu.SemaphoreType.DMA((4,)),
        ],
        name="edges",
    )(field)


def march_body(
    offsets, table, field_hbm, mats_hbm, z_first, z_second, y_first, y_second,
    first, own, spill, field, mats, weight, keep, spread, halves, sems,
):
    depth, rows, width = field_hbm.shape
    strips = width // LANES
    groups = rows // GROUP
    cols = [slice(j * LANES, (j + 1) * LANES) for j in range(strips)]

    def arrivals(kind, g):
        start = g * GROUP
        for j in range(strips):
            lanes = pl.ds(j * LANES, LANES)
            if kind == 0:
                yield pltpu.make_async_copy(
                    field_hbm.at[:, pl.ds(start, GROUP), lanes],
                    field.at[pl.ds(1, depth), j, pl.ds(SUB + start, GROUP), :],
                    sems.at[0, g, j],
                )
            else:
                yield pltpu.make_async_copy(
                    mats_hbm.at[:, pl.ds(start, GROUP), lanes],
                    mats.at[:, j, pl.ds(start, GROUP), :],
                    sems.at[1, g, j],
                )

    for g in range(groups):
        for kind in range(2):
            for copy in arrivals(kind, g):
                copy.start()
    z_even, y_even = is_even("depth"), is_even("area")
    first_plane = jnp.where(z_even, depth + 1, 0)
    second_plane = jnp.where(z_even, 0, depth + 1)
    for j in range(strips):
        field[first_plane, j, SUB : SUB + rows, :] = z_first[:, cols[j]]
        field[second_plane, j, SUB : SUB + rows, :] = z_second[:, cols[j]]
        one, two = y_first[:, cols[j]], y_second[:, cols[j]]
        field[1 : depth + 1, j, SUB - 1, :] = jnp.where(y_even, two, one)
        field[1 : depth + 1, j, SUB + rows, :] = jnp.where(y_even, one, two)
    spread[...] = jnp.zeros_like(spread)
    lane = lax.broadcasted_iota(jnp.int32, (SUB, LANES), 1)
    entry = lax.broadcasted_iota(jnp.int32, (SUB, LANES), 0)
    left_end = lane == 0
    right_end = lane == LANES - 1
    zero = jnp.zeros((SUB, LANES), jnp.float32)
    for c in range(4):
        for half in range(2):
            rows_of = zero
            for e in range(SUB):
                rows_of = jnp.where(entry == e, table[c, half * SUB + e], rows_of)
            halves[c, half] = rows_of if c == 3 else SHADE_UNIT * rows_of
    shift = offsets[lax.axis_index("depth")]

    def table_of(c):
        return halves[c, 0], halves[c, 1]

    def tile(i, unused):
        r = pl.multiple_of(i * SUB, SUB)

        def cells(z, unused):
            f = [field[z + 1, j, pl.ds(SUB + r, SUB), :] for j in range(strips)]
            from_left = [pltpu.roll(v, 1, 1) for v in f]
            from_right = [pltpu.roll(v, LANES - 1, 1) for v in f]
            for j in range(strips):
                above = field[z + 2, j, pl.ds(SUB + r, SUB), :]
                below = field[z, j, pl.ds(SUB + r, SUB), :]
                dz = above - below
                dy = (
                    field[z + 1, j, pl.ds(SUB + r + 1, SUB), :]
                    - field[z + 1, j, pl.ds(SUB + r - 1, SUB), :]
                )
                left = jnp.where(left_end, from_left[j - 1] if j else zero, from_left[j])
                right = jnp.where(
                    right_end, from_right[j + 1] if j < strips - 1 else zero, from_right[j]
                )
                dx = right - left
                grad_sq = 0.25 * (dz * dz + dy * dy + dx * dx)
                slope = jnp.abs(dz + (0.6 / 0.48) * dy + (0.64 / 0.48) * dx)
                shade = (0.3 / SHADE_UNIT) + slope * lax.rsqrt(grad_sq + 1.0)
                clear = jnp.exp2((-0.25 * LOG2E) * (f[j] * f[j] + grad_sq))
                most = lookup(table_of(3), mats[z, j, pl.ds(r, SUB), :])
                opacity = most - most * clear
                weight[z, j] = shade * opacity
                keep[z, j] = 1.0 - opacity
            return unused

        lax.fori_loop(0, depth, cells, 0, unroll=16)
        for j0 in range(0, strips, 2):
            colours = [table_of(c) for c in range(3)]

            def step(z, carry):
                result = []
                for k, (passed, front, back) in enumerate(carry):
                    j = j0 + k
                    w = weight[z, j]
                    kept = keep[z, j]
                    seen = w * passed
                    idx = mats[z, j, pl.ds(r, SUB), :]
                    looked = [lookup(t, idx) for t in colours]
                    result.append(
                        (
                            passed * kept,
                            [front[c] + looked[c] * seen for c in range(3)],
                            [back[c] * kept + looked[c] * w for c in range(3)],
                        )
                    )
                return result

            start = [(zero + 1.0, [zero] * 3, [zero] * 3)] * 2
            done = lax.fori_loop(0, depth, step, start, unroll=16)
            for k, (passed, front, back) in enumerate(done):
                j = j0 + k
                place = pl.ds(shift + r, SUB)
                for c in range(3):
                    put(first, i, c, cols[j], front[c])
                    spread[c, j, place, :] = back[c]
                put(first, i, 3, cols[j], 1.0 - passed)
                spread[3, j, place, :] = 1.0 - passed
        return unused

    for copy in arrivals(0, 0):
        copy.wait()

    def group(g, unused):
        for copy in arrivals(1, g):
            copy.wait()

        @pl.when(g + 1 < groups)
        def _():
            for copy in arrivals(0, g + 1):
                copy.wait()

        return lax.fori_loop(g * (GROUP // SUB), (g + 1) * (GROUP // SUB), tile, unused)

    lax.fori_loop(0, groups, group, 0)

    def hand_out(i, unused):
        r = pl.multiple_of(i * SUB, SUB)
        for c in range(4):
            for j in range(strips):
                put(own, i, c, cols[j], spread[c, j, pl.ds(r, SUB), :])
                put(spill, i, c, cols[j], spread[c, j, pl.ds(rows + r, SUB), :])
        return unused

    lax.fori_loop(0, rows // SUB, hand_out, 0)


def march(offsets, table, field, mats, rims, receivers):
    depth, rows, width = field.shape
    strips = width // LANES
    vmem = pl.BlockSpec(memory_space=pltpu.VMEM)
    smem = pl.BlockSpec(memory_space=pltpu.SMEM)
    hbm = pl.BlockSpec(memory_space=pltpu.HBM)
    image = jax.ShapeDtypeStruct((receivers, 4, rows // receivers, width), jnp.float32)
    return pl.pallas_call(
        march_body,
        out_shape=(image, image, image),
        in_specs=[smem, smem, hbm, hbm] + [vmem] * 4,
        out_specs=(vmem, vmem, vmem),
        scratch_shapes=[
            pltpu.VMEM((depth + 2, strips, rows + 2 * SUB, LANES), jnp.float32),
            pltpu.VMEM((depth, strips, rows, LANES), jnp.int32),
            pltpu.VMEM((depth, strips, SUB, LANES), jnp.float32),
            pltpu.VMEM((depth, strips, SUB, LANES), jnp.float32),
            pltpu.VMEM((4, strips, 2 * rows, LANES), jnp.float32),
            pltpu.VMEM((4, 2, SUB, LANES), jnp.float32),
            pltpu.SemaphoreType.DMA((2, rows // GROUP, strips)),
        ],
        cost_estimate=pl.CostEstimate(flops=10**8, bytes_accessed=10**7, transcendentals=10**6),
        name="march",
    )(offsets, table, field, mats, *rims)


def composite_body(order, stack, out):
    layers = stack.shape[0]
    for view in range(out.shape[0]):
        seen = jnp.ones(stack.shape[2:], jnp.float32)
        colour = [jnp.zeros(stack.shape[2:], jnp.float32)] * 3
        for k in range(layers):
            layer = order[view, k]
            colour = [colour[c] + seen * stack[layer, 4 * view + c] for c in range(3)]
            seen = seen - seen * stack[layer, 4 * view + 3]
        for c in range(3):
            out[view, c] = colour[c]
        out[view, 3] = 1.0 - seen


def composite(order, stack):
    vmem = pl.BlockSpec(memory_space=pltpu.VMEM)
    return pl.pallas_call(
        composite_body,
        out_shape=jax.ShapeDtypeStruct((2, 4) + stack.shape[2:], jnp.float32),
        in_specs=[pl.BlockSpec(memory_space=pltpu.SMEM), vmem],
        out_specs=vmem,
        name="composite",
    )(order, stack)


def swapped(block, axis, start):
    pairs = [(i, i + 1) for i in range(start, lax.axis_size(axis) - 1, 2)]
    return lax.ppermute(block, axis, pairs + [(b, a) for a, b in pairs])


def shards(field, materials, tf_table, view_order, shear_offset):
    receivers = lax.axis_size("depth")
    z_first, z_second, y_first, y_second = edges(field)
    rims = (
        swapped(z_first, "depth", 0),
        swapped(z_second, "depth", 1),
        swapped(y_first, "area", 0),
        swapped(y_second, "area", 1),
    )
    first, own, spill = march(shear_offset, tf_table, field, materials, rims, receivers)
    columns = lax.axis_size("area")
    arrived = lax.ppermute(spill, "area", [(i, i + 1) for i in range(columns - 1)])
    both = jnp.concatenate([first, own + arrived], axis=1)
    stack = lax.all_to_all(both, "depth", split_axis=0, concat_axis=0, tiled=True)
    return composite(view_order, stack)


def solution(mesh):
    in_specs = (P("depth", "area", None), P("depth", "area", None), P(), P(), P())
    out_specs = P(None, None, ("area", "depth"), None)
    return jax.shard_map(shards, mesh=mesh, in_specs=in_specs, out_specs=out_specs, check_vma=False)
```

time: 85 us -> 69.7 us (0.82)
  the two profiles are of different devices: /device:TPU:0 before, /device:TPU:1 now
where the time goes in v1:
time: 69.7 us; the launch traced here: 69.4 us
  blocking collectives  28.6 us (41%)
  Pallas kernels  18 us (26%)
  starting transfers between devices  9.87 us (14%)
  waiting for transfers between devices  9.14 us (13%)
  other arithmetic  2.26 us (3%)
  local copies, waits for them, and re-layouts  1.31 us (2%)
    all_to_all x1, blocking collectives, shards(): lax.all_to_all(both, 'depth', split_axis=0, concat_axis=0, tiled=True)  28.6 us
    pallas_call x1, Pallas kernels, march(): pl.pallas_call(march_body, out_shape=(image, image, image), in_specs=[sme...  13.9 us
    ppermute x4, starting transfers between devices, swapped(): return lax.ppermute(block, axis, pairs + [(b, a) for a, b in pairs])  6.82 us
    ppermute x1, waiting for transfers between devices, shards(): lax.ppermute(spill, 'area', [(i, i + 1) for i in range(columns - 1)])  6.42 us
    ppermute x1, starting transfers between devices, shards(): lax.ppermute(spill, 'area', [(i, i + 1) for i in range(columns - 1)])  3.06 us
    ppermute x4, waiting for transfers between devices, swapped(): return lax.ppermute(block, axis, pairs + [(b, a) for a, b in pairs])  2.72 us
    pallas_call x1, Pallas kernels, edges(): pl.pallas_call(edges_body, out_shape=(plane, plane, wall, wall), in_specs...  2.15 us
    pallas_call x1, Pallas kernels, composite(): pl.pallas_call(composite_body, out_shape=jax.ShapeDtypeStruct((2, 4) + st...  1.96 us
  transfers between devices with their start and end apart: 5, of which 2 were waited for; matrix products, arithmetic and copies ran while one was open for 0% of the time, Pallas kernels for 0%

profile of v1, /device:TPU:1, one launch (start us, length us, event | category | flops | bytes accessed | tf_op | source)
XLA Modules:
  0.0 69.4 jit_solution(8650155774246520621)
XLA Ops:
  0.0 2.2 %edges.1 = (f32[64,512]{1,0:T(8,128)}, f32[64,512]{1,0:T(8,128)}, f32[32,512]{1,0:T(8,128)}, f32[32,512]{1,0:T(8,128)}) custom-call(f32[32,64,512]{2,1,0:T(8,128)} %field_hbm.3), custom_call_target="tpu_custom_call" | custom-call | tf_op jit(solution)/shard_map/edges/pallas_call | solution.py:74
  2.2 2.1 %collective-permute-start = (f32[64,512]{1,0:T(8,128)}, f32[64,512]{1,0:T(8,128)S(1)}, u32[]{:S(2)}, u32[]{:S(2)}) collective-permute-start(f32[64,512]{1,0:T(8,128)} %get-tuple-element.12), channel_id=1, source_target_pairs={{0,1},{2,3},{4,5},{6,7},{1,0},{3,2},{5,4},{7,6},{8,9},{10,11},{12,... | collective-permute-start | bytes 393224 | tf_op jit(solution)/shard_map/ppermute | solution.py:287
  4.3 0.7 collective-permute-start.1
  4.9 1.0 %collective-permute-start.2 = (f32[32,512]{1,0:T(8,128)}, f32[32,512]{1,0:T(8,128)S(1)}, u32[]{:S(2)}, u32[]{:S(2)}) collective-permute-start(f32[32,512]{1,0:T(8,128)} %get-tuple-element.14), channel_id=1, source_target_pairs={{0,8},{16,24},{8,0},{24,16},{1,9},{17,25},{9,1},{25,17},{2,10},{18... | collective-permute-start | bytes 196616 | tf_op jit(solution)/shard_map/ppermute | solution.py:287
  5.9 3.0 %collective-permute-start.3 = (f32[32,512]{1,0:T(8,128)}, f32[32,512]{1,0:T(8,128)S(1)}, u32[]{:S(2)}, u32[]{:S(2)}) collective-permute-start(f32[32,512]{1,0:T(8,128)} %get-tuple-element.15), channel_id=1, source_target_pairs={{8,16},{16,8},{9,17},{17,9},{10,18},{18,10},{11,19},{19,11},{12,20... | collective-permute-start | bytes 196616 | tf_op jit(solution)/shard_map/ppermute | solution.py:287
  9.0 0.0 collective-permute-done.2.y_first
  9.0 0.0 copy-start.2
  9.0 2.7 %collective-permute-done.3.y_second = f32[32,512]{1,0:T(8,128)S(1)} collective-permute-done((f32[32,512]{1,0:T(8,128)}, f32[32,512]{1,0:T(8,128)S(1)}, u32[]{:S(2)}, u32[]{:S(2)}) %collective-permute-start.3) | collective-permute-done | bytes 65568 | tf_op jit(solution)/shard_map/ppermute | solution.py:287
  11.7 0.0 copy-start.3
  11.7 0.0 collective-permute-done.z_first
  11.7 0.0 copy-start
  11.7 0.0 collective-permute-done.1.z_second
  11.7 0.0 copy-done.2
  11.7 0.6 copy-done.3
  12.4 0.0 copy-done
  12.4 0.0 copy-start.1
  12.4 0.6 copy-done.1
  13.1 13.9 %march.1 = (f32[8,4,8,512]{3,2,1,0:T(8,128)}, f32[8,4,8,512]{3,2,1,0:T(8,128)}, f32[8,4,8,512]{3,2,1,0:T(8,128)}) custom-call(s32[8]{0:T(128)} %offsets.1, f32[4,16]{1,0:T(4,128)} %table.1, f32[32,64,512]{2,1,0:T(8,128)} %field_hbm.3, s32[32,64,512]{2,1,0:T(8,128)} %mats_hbm.1, f32[64,512]{1,0:T(8,128)} %copy-done, f32[64,512]{1,0:T(8,128)} %copy-done.1, ...), custom_call_target="tpu_custom_call" | custom-call | flops 100000000 | bytes 10000000 | tf_op jit(solution)/shard_map/march/pallas_call | solution.py:241
  27.0 3.1 %collective-permute-start.4 = (f32[8,4,8,512]{3,2,1,0:T(8,128)}, f32[8,4,8,512]{3,2,1,0:T(8,128)S(1)}, u32[]{:S(2)}, u32[]{:S(2)}) collective-permute-start(f32[8,4,8,512]{3,2,1,0:T(8,128)} %get-tuple-element.18), channel_id=1, source_target_pairs={{0,8},{8,16},{16,24},{1,9},{9,17},{17,25},{2,10},{10,18},{18,26},{... | collective-permute-start | bytes 1572872 | tf_op jit(solution)/shard_map/ppermute | solution.py:301
  30.1 6.4 %collective-permute-done.4 = f32[8,4,8,512]{3,2,1,0:T(8,128)S(1)} collective-permute-done((f32[8,4,8,512]{3,2,1,0:T(8,128)}, f32[8,4,8,512]{3,2,1,0:T(8,128)S(1)}, u32[]{:S(2)}, u32[]{:S(2)}) %collective-permute-start.4) | collective-permute-done | bytes 524320 | tf_op jit(solution)/shard_map/ppermute | solution.py:301
  36.5 1.1 %add.3 = f32[8,4,8,512]{3,2,1,0:T(8,128)S(1)} add(f32[8,4,8,512]{3,2,1,0:T(8,128)} %get-tuple-element.17, f32[8,4,8,512]{3,2,1,0:T(8,128)S(1)} %collective-permute-done.4) | non-fusion elementwise | flops 131072 | bytes 1572864 | tf_op jit(solution)/shard_map/add | solution.py:302
  37.6 1.1 %pad_maximum_fusion = f32[8,8,8,512]{3,2,1,0:T(8,128)S(1)} fusion(f32[8,4,8,512]{3,2,1,0:T(8,128)S(1)} %add.3, f32[8,4,8,512]{3,2,1,0:T(8,128)} %get-tuple-element.16), kind=kLoop, calls=%fused_computation | loop fusion | flops 262144 | bytes 2097152 | tf_op jit(solution)/shard_map/concatenate | solution.py:302
  38.8 28.6 %all_to_all.5.stack = f32[8,8,8,512]{3,2,1,0:T(8,128)} all-to-all(f32[8,8,8,512]{3,2,1,0:T(8,128)S(1)} %pad_maximum_fusion), channel_id=1, replica_groups=mesh['area'=4,'depth'=8] {'depth'}, dimensions={0} | all-to-all | bytes 2097152 | tf_op jit(solution)/shard_map/all_to_all | solution.py:303
  67.4 2.0 %composite.1 = f32[2,4,8,512]{3,2,1,0:T(8,128)} custom-call(s32[2,8]{1,0:T(2,128)} %order.1, f32[8,8,8,512]{3,2,1,0:T(8,128)} %all_to_all.5.stack), custom_call_target="tpu_custom_call" | custom-call | tf_op jit(solution)/shard_map/composite/pallas_call | solution.py:276
Async XLA Ops:
  2.2 9.6 %collective-permute-start = (f32[64,512]{1,0:T(8,128)}, f32[64,512]{1,0:T(8,128)S(1)}, u32[]{:S(2)}, u32[]{:S(2)}) collective-permute-start(f32[64,512]{1,0:T(8,128)} %get-tuple-element.12), channel_id=1, source_target_pairs={{0,1},{2,3},{4,5},{6,7},{1,0},{3,2},{5,4},{7,6},{8,9},{10,11},{12,... | collective-permute-start | bytes 393224 | tf_op jit(solution)/shard_map/ppermute | solution.py:287
  4.3 7.5 %collective-permute-start.1 = (f32[64,512]{1,0:T(8,128)}, f32[64,512]{1,0:T(8,128)S(1)}, u32[]{:S(2)}, u32[]{:S(2)}) collective-permute-start(f32[64,512]{1,0:T(8,128)} %get-tuple-element.13), channel_id=1, source_target_pairs={{1,2},{3,4},{5,6},{2,1},{4,3},{6,5},{9,10},{11,12},{13,14},{10,9},... | collective-permute-start | bytes 393224 | tf_op jit(solution)/shard_map/ppermute | solution.py:287
  4.9 4.1 %collective-permute-start.2 = (f32[32,512]{1,0:T(8,128)}, f32[32,512]{1,0:T(8,128)S(1)}, u32[]{:S(2)}, u32[]{:S(2)}) collective-permute-start(f32[32,512]{1,0:T(8,128)} %get-tuple-element.14), channel_id=1, source_target_pairs={{0,8},{16,24},{8,0},{24,16},{1,9},{17,25},{9,1},{25,17},{2,10},{18... | collective-permute-start | bytes 196616 | tf_op jit(solution)/shard_map/ppermute | solution.py:287
  5.9 5.8 %collective-permute-start.3 = (f32[32,512]{1,0:T(8,128)}, f32[32,512]{1,0:T(8,128)S(1)}, u32[]{:S(2)}, u32[]{:S(2)}) collective-permute-start(f32[32,512]{1,0:T(8,128)} %get-tuple-element.15), channel_id=1, source_target_pairs={{8,16},{16,8},{9,17},{17,9},{10,18},{18,10},{11,19},{19,11},{12,20... | collective-permute-start | bytes 196616 | tf_op jit(solution)/shard_map/ppermute | solution.py:287
  9.0 2.7 %copy-start.2 = (f32[32,512]{1,0:T(8,128)}, f32[32,512]{1,0:T(8,128)S(1)}, u32[]{:S(2)}) copy-start(f32[32,512]{1,0:T(8,128)S(1)} %collective-permute-done.2.y_first) | copy-start | bytes 196612
  11.7 0.6 copy-start.3
  11.7 0.7 copy-start
  12.4 0.7 copy-start.1
  27.0 9.5 %collective-permute-start.4 = (f32[8,4,8,512]{3,2,1,0:T(8,128)}, f32[8,4,8,512]{3,2,1,0:T(8,128)S(1)}, u32[]{:S(2)}, u32[]{:S(2)}) collective-permute-start(f32[8,4,8,512]{3,2,1,0:T(8,128)} %get-tuple-element.18), channel_id=1, source_target_pairs={{0,8},{8,16},{16,24},{1,9},{9,17},{17,25},{2,10},{10,18},{18,26},{... | collective-permute-start | bytes 1572872 | tf_op jit(solution)/shard_map/ppermute | solution.py:301
